TPU v7x, 32 devices: a whole 2x2x4 slice. The times are simulated.
32 devices in a mesh: groups: 2 (over y), seq: 4 (over z), head: 4 (over x, core).
Axes of the slice: x: 2, y: 2, z: 4, core: 2. Of those that a mesh axis runs over, the one named last changes fastest.
Arguments:
- queries: bfloat16 [8, 2, 64, 128], P(('groups', 'seq'), None, 'head'), parts along dimension 0, may hold values from -128 to 128
- new_keys: bfloat16 [8, 2, 8, 128], P(('groups', 'seq'), None, 'head'), parts along dimension 0, may hold values from -24 to 24
- new_values: bfloat16 [8, 2, 8, 128], P(('groups', 'seq'), None, 'head'), parts along dimension 0, may hold values from -6 to 6
- shared_keys: bfloat16 [2048, 8, 128], P(('groups', 'seq'), 'head'), parts along dimension 0, may hold values from -4 to 4
- shared_values: bfloat16 [2048, 8, 128], P(('groups', 'seq'), 'head'), parts along dimension 0, may hold values from -6 to 6
- fewshot_keys: bfloat16 [4096, 8, 128], P(('groups', 'seq'), 'head'), parts along dimension 0, may hold values from -9 to 9
- fewshot_values: bfloat16 [4096, 8, 128], P(('groups', 'seq'), 'head'), parts along dimension 0, may hold values from -6 to 6
- suffix_keys: bfloat16 [16, 128, 8, 128], P(('groups', 'seq'), None, 'head'), parts along dimension 0, may hold values from -12 to 12
- suffix_values: bfloat16 [16, 128, 8, 128], P(('groups', 'seq'), None, 'head'), parts along dimension 0, may hold values from -6 to 6
- request_prefix: int32 [8], P('groups'), parts along dimension 0, may hold values from 0 to 3, as said below
- prefix_owner: int32 [8], P('groups'), parts along dimension 0, may hold values from 0 to 3, each once
- prefix_length: int32 [8], P('groups'), parts along dimension 0, may hold values from 128 to 512, as said below
- suffix_slot: int32 [8], P('groups'), parts along dimension 0, may hold values from 0 to 7, as said below
- suffix_length: int32 [8], P('groups'), parts along dimension 0, may hold values from 1 to 128, as said below
Outputs:
- attn: bfloat16 [8, 2, 64, 128], P(('groups', 'seq'), None, 'head'), parts along dimension 0
There are 2 independent parts, one for each index of `groups`. A program takes and returns all parts, laid end to end along the dimension named above; each array names one. Nothing has to cross between parts.
Inputs may be any that keep to these rules, and one draw needn't show every extreme that they name: `request_prefix`: no prefix is used by more than 2 requests; some prefix by exactly 2. `prefix_length`: the longest prefix has exactly 512 positions. `suffix_slot`: distinct for distinct requests; slot s lies on index s // 2 of seq; some index of seq holds exactly 2 requests' suffixes. `suffix_length`: the longest suffix has exactly 128 positions.
All inputs are finite; a program needn't handle non-finite values.
Results may differ from a plain program's by a relative error of at most 0.004.
Values may be sent and summed in bfloat16 or wider, within the bound.
A program may use at most 64 MiB of HBM per device.

v0:
```python
import jax
import jax.numpy as jnp
from jax import lax
from jax.sharding import PartitionSpec as P

very_low = -1e30


def block_attend(rows_in, keys_in, values_in, lengths):
    batch_rows, groups_kv, per_group, head_width = rows_in.shape
    length = keys_in.shape[0]
    block_len = min(length, 256)
    blocks = length // block_len
    inv_root = head_width ** (-0.5)
    key_blocks = keys_in.reshape(blocks, block_len, groups_kv, head_width)
    value_blocks = values_in.reshape(blocks, block_len, groups_kv, head_width)
    starts = jnp.arange(blocks, dtype=jnp.int32) * block_len
    offsets = jnp.arange(block_len, dtype=jnp.int32)

    def advance(running, inputs):
        highest, totals, weighted = running
        key_part, value_part, first_pos = inputs
        scores = (
            jnp.einsum("bgqd,lgd->bgql", rows_in, key_part, preferred_element_type=jnp.float32)
            * inv_root
        )
        usable = ((first_pos + offsets)[None, :] < lengths[:, None])[:, None, None, :]
        scores = jnp.where(usable, scores, very_low)
        new_high = jnp.maximum(highest, jnp.max(scores, axis=-1))
        weights = jnp.where(usable, jnp.exp(scores - new_high[..., None]), 0.0)
        factor = jnp.exp(highest - new_high)
        totals = totals * factor + jnp.sum(weights, axis=-1)
        weighted = weighted * factor[..., None] + jnp.einsum(
            "bgql,lgd->bgqd",
            weights.astype(jnp.bfloat16),
            value_part,
            preferred_element_type=jnp.float32,
        )
        return ((new_high, totals, weighted), None)

    start_state = (
        jnp.full((batch_rows, groups_kv, per_group), very_low, jnp.float32),
        jnp.zeros((batch_rows, groups_kv, per_group), jnp.float32),
        jnp.zeros((batch_rows, groups_kv, per_group, head_width), jnp.float32),
    )
    result, unused = lax.scan(advance, start_state, (key_blocks, value_blocks, starts))
    return result


def slot_attend(rows_in, keys_in, values_in, usable):
    inv_root = rows_in.shape[-1] ** (-0.5)
    scores = (
        jnp.einsum("ctgqd,clgd->ctgql", rows_in, keys_in, preferred_element_type=jnp.float32)
        * inv_root
    )
    mask_all = usable[:, :, None, None, :]
    scores = jnp.where(mask_all, scores, very_low)
    highest = jnp.max(scores, axis=-1)
    weights = jnp.where(mask_all, jnp.exp(scores - highest[..., None]), 0.0)
    totals = jnp.sum(weights, axis=-1)
    weighted = jnp.einsum(
        "ctgql,clgd->ctgqd",
        weights.astype(jnp.bfloat16),
        values_in,
        preferred_element_type=jnp.float32,
    )
    return (highest, totals, weighted)


def combine(first_part, second_part):
    high_a, total_a, sum_a = first_part
    high_b, total_b, sum_b = second_part
    highest = jnp.maximum(high_a, high_b)
    factor_a = jnp.exp(high_a - highest)
    factor_b = jnp.exp(high_b - highest)
    return (
        highest,
        total_a * factor_a + total_b * factor_b,
        sum_a * factor_a[..., None] + sum_b * factor_b[..., None],
    )


def spread(partial_value, picks):
    highest, totals, weighted = partial_value
    lifted = jnp.max(jnp.where(picks[:, :, None, None, None], highest[None], very_low), axis=1)
    onehot_rows = picks.astype(jnp.float32)
    totals = jnp.einsum("rc,ctgq->rtgq", onehot_rows, totals, precision=lax.Precision.HIGHEST)
    weighted = jnp.einsum("rc,ctgqd->rtgqd", onehot_rows, weighted, precision=lax.Precision.HIGHEST)
    return (lifted, totals, weighted)


def fold_sources(parts_in):
    highest, totals, weighted = parts_in
    top_all = jnp.max(highest, axis=0)
    factor = jnp.exp(highest - top_all)
    return (
        top_all,
        jnp.sum(totals * factor, axis=0),
        jnp.sum(weighted * factor[..., None], axis=0),
    )


def per_device(
    queries,
    new_keys,
    new_values,
    shared_keys,
    shared_values,
    fewshot_keys,
    fewshot_values,
    suffix_keys,
    suffix_values,
    request_prefix,
    prefix_owner,
    prefix_length,
    suffix_slot,
    suffix_length,
):
    devices_seq = lax.axis_size("seq")
    my_index = lax.axis_index("seq")
    req_dev, step_count, heads_local, head_width = queries.shape
    kv_local = new_keys.shape[2]
    group_size = heads_local // kv_local
    requests = req_dev * devices_seq
    request_ids = jnp.arange(requests, dtype=jnp.int32)
    gathered = lax.all_gather(queries, "seq", axis=0, tiled=True)
    query_rows = gathered.reshape(requests * step_count, kv_local, group_size, head_width)
    everyone = jnp.full((requests * step_count,), shared_keys.shape[0], jnp.int32)
    shared_part = block_attend(query_rows, shared_keys, shared_values, everyone)
    shared_part = tuple(
        (item.reshape((requests, step_count) + item.shape[1:]) for item in shared_part)
    )
    prefixes = prefix_owner.shape[0]
    chooser = request_prefix[:, None] == jnp.arange(prefixes, dtype=jnp.int32)[None, :]
    home_slot = jnp.sum(jnp.where(chooser, prefix_owner[None, :], 0), axis=1)
    use_here = home_slot == my_index
    own_length = jnp.sum(jnp.where(prefix_owner == my_index, prefix_length, 0))
    row_lengths = jnp.repeat(jnp.where(use_here, own_length, 0), step_count)
    few_part = block_attend(query_rows, fewshot_keys, fewshot_values, row_lengths)
    few_part = tuple((item.reshape((requests, step_count) + item.shape[1:]) for item in few_part))
    running = combine(shared_part, few_part)
    slot_count = suffix_keys.shape[0]
    my_slots = my_index * slot_count + jnp.arange(slot_count, dtype=jnp.int32)
    owned = suffix_slot[:, None] == my_slots[None, :]
    holder = jnp.sum(jnp.where(owned, request_ids[:, None], 0), axis=0)
    slot_length = jnp.sum(jnp.where(owned, suffix_length[:, None], 0), axis=0)
    slot_rows = jnp.take(gathered, holder, axis=0).reshape(
        slot_count, step_count, kv_local, group_size, head_width
    )
    positions = jnp.arange(suffix_keys.shape[1], dtype=jnp.int32)
    slot_usable = jnp.broadcast_to(
        (positions[None, :] < slot_length[:, None])[:, None, :],
        (slot_count, step_count, suffix_keys.shape[1]),
    )
    suffix_part = slot_attend(slot_rows, suffix_keys, suffix_values, slot_usable)
    highest, totals, weighted = combine(running, spread(suffix_part, owned))
    merged = fold_sources(
        (
            lax.all_to_all(highest[None], "seq", split_axis=1, concat_axis=0, tiled=True),
            lax.all_to_all(totals[None], "seq", split_axis=1, concat_axis=0, tiled=True),
            lax.all_to_all(weighted[None], "seq", split_axis=1, concat_axis=0, tiled=True),
        )
    )
    own_rows = queries.reshape(req_dev, step_count, kv_local, group_size, head_width)
    step_pos = jnp.arange(step_count, dtype=jnp.int32)
    causal = (step_pos[:, None] >= step_pos[None, :])[None]
    new_part = slot_attend(own_rows, new_keys, new_values, causal)
    final_top, final_totals, final_weighted = combine(merged, new_part)
    output = final_weighted / final_totals[..., None]
    return output.reshape(req_dev, step_count, heads_local, head_width).astype(jnp.bfloat16)


def solution(mesh):
    return jax.shard_map(
        per_device,
        mesh=mesh,
        in_specs=(
            P(("groups", "seq"), None, "head", None),
            P(("groups", "seq"), None, "head", None),
            P(("groups", "seq"), None, "head", None),
            P(("groups", "seq"), "head", None),
            P(("groups", "seq"), "head", None),
            P(("groups", "seq"), "head", None),
            P(("groups", "seq"), "head", None),
            P(("groups", "seq"), None, "head", None),
            P(("groups", "seq"), None, "head", None),
            P("groups"),
            P("groups"),
            P("groups"),
            P("groups"),
            P("groups"),
        ),
        out_specs=P(("groups", "seq"), None, "head", None),
        check_vma=False,
    )
```

profile of v0, /device:TPU:0, one launch (start us, length us, event | category | flops | bytes accessed | tf_op | source)
XLA Modules:
  0.0 57.3 jit_solution(15646962048108506949)
XLA Ops:
  0.1 0.6 %copy-done.2 = s32[4]{0:T(128)S(1)} copy-done((s32[4]{0:T(128)S(1)}, s32[4]{0:T(128)}, u32[]{:S(2)}) %copy-start.2) | copy-done | bytes 40
  0.7 0.2 select_reduce_fusion.3
  0.9 14.9 %all_gather.3 = bf16[4,2,16,128]{3,2,1,0:T(8,128)(2,1)S(1)} all-gather(bf16[1,2,16,128]{3,2,1,0:T(8,128)(2,1)S(1)} %copy-done.1), channel_id=1, replica_groups=mesh['groups'=2,'seq'=4,'head'=4] {'seq'}, dimensions={0}, use_global_device_ids=true | all-gather | bytes 40960 | tf_op jit(solution)/shard_map/all_gather | solution.py:126
  15.8 0.6 %copy-done.4 = s32[4]{0:T(128)S(1)} copy-done((s32[4]{0:T(128)S(1)}, s32[4]{0:T(128)}, u32[]{:S(2)}) %copy-start.4) | copy-done | bytes 40
  16.5 0.2 select_reduce_fusion.1
  16.7 0.5 copy-done.5
  17.1 0.7 %fusion.70 = s32[]{:T(128)} fusion(s32[4]{0:T(128)S(1)} %copy-done.5, s32[4]{0:T(128)S(1)} %copy-done.4, s32[]{:T(128)S(6)} %axis_index.15), kind=kLoop, calls=%fused_computation.127 | loop fusion | flops 11 | bytes 40 | tf_op jit(solution)/shard_map/reduce_sum | solution.py:137
  17.8 0.7 %compare_select_fusion.3 = s32[4]{0:T(128)S(1)} fusion(s32[4]{0:T(128)S(1)} %select_reduce_fusion.1, s32[]{:T(128)} %fusion.70, s32[]{:T(128)S(6)} %axis_index.15), kind=kLoop, calls=%fused_computation.119 | loop fusion | flops 8 | bytes 40 | tf_op jit(solution)/shard_map/jit(_where)/select_n | solution.py:138
  18.6 7.0 %while.3 = (s32[]{:T(128)}, f32[8,2,8]{2,0,1:T(8,128)S(1)}, f32[8,2,8]{2,0,1:T(8,128)S(1)}, f32[8,2,8,128]{3,2,0,1:T(8,128)S(1)}, s32[2]{0:T(128)S(1)}, /*index=...) while((s32[]{:T(128)}, f32[8,2,8]{2,0,1:T(8,128)S(1)}, ...), condition=%wide.region_6.7_spmd.clone, body=%wide.region_3.6_spmd.clone.sunk | while | flops 17124228 | bytes 1362213 | solution.py:46
  18.6 1.2 %constant_dynamic-slice_fusion.3 = (bf16[1,256,2,128]{3,2,1,0:T(2,128)(2,1)S(1)}, bf16[1,256,2,128]{3,2,1,0:T(2,128)(2,1)S(1)}) fusion(bf16[2,256,2,128]{3,2,1,0:T(2,128)(2,1)} %get-tuple-element.305, s32[]{:T(128)S(6)} %copy.452, bf16[2,256,2,128]{3,2,1,0:T(2,128)(2,1)} %get-tuple-element.303), kind=kLoop, calls=%fused_computation.23.clone.1 | loop fusion | bytes 524292 | tf_op jit(solution)/shard_map/while/body/jit(dynamic_index_in_dim)/dynamic_slice | solution.py:46
  19.8 0.7 %dynamic_slice.27 = s32[1]{0:T(128)} dynamic-slice(s32[2]{0:T(128)S(1)} %get-tuple-element.302, s32[]{:T(128)S(6)} %copy.452), dynamic_slice_sizes={1} | dynamic-slice | bytes 12 | tf_op jit(solution)/shard_map/while/body/jit(dynamic_index_in_dim)/dynamic_slice | solution.py:46
  20.4 0.7 %iota_add_fusion.3 = s32[256]{0:T(256)S(1)} fusion(s32[]{:T(128)} %bitcast.146), kind=kLoop, calls=%fused_computation.22.clone.1 | loop fusion | flops 256 | bytes 1028 | tf_op jit(solution)/shard_map/while/body/eval_jaxpr/add | solution.py:27
  21.4 0.3 fusion.94
  21.6 0.2 fusion.95
  21.8 0.2 fusion.97
  22.1 1.2 %constant_dynamic-slice_fusion.3 = (bf16[1,256,2,128]{3,2,1,0:T(2,128)(2,1)S(1)}, bf16[1,256,2,128]{3,2,1,0:T(2,128)(2,1)S(1)}) fusion(bf16[2,256,2,128]{3,2,1,0:T(2,128)(2,1)} %get-tuple-element.305, s32[]{:T(128)S(6)} %copy.452, bf16[2,256,2,128]{3,2,1,0:T(2,128)(2,1)} %get-tuple-element.303), kind=kLoop, calls=%fused_computation.23.clone.1 | loop fusion | bytes 524292 | tf_op jit(solution)/shard_map/while/body/jit(dynamic_index_in_dim)/dynamic_slice | solution.py:46
  23.2 0.7 %dynamic_slice.27 = s32[1]{0:T(128)} dynamic-slice(s32[2]{0:T(128)S(1)} %get-tuple-element.302, s32[]{:T(128)S(6)} %copy.452), dynamic_slice_sizes={1} | dynamic-slice | bytes 12 | tf_op jit(solution)/shard_map/while/body/jit(dynamic_index_in_dim)/dynamic_slice | solution.py:46
  23.9 0.7 %iota_add_fusion.3 = s32[256]{0:T(256)S(1)} fusion(s32[]{:T(128)} %bitcast.146), kind=kLoop, calls=%fused_computation.22.clone.1 | loop fusion | flops 256 | bytes 1028 | tf_op jit(solution)/shard_map/while/body/eval_jaxpr/add | solution.py:27
  24.8 0.3 fusion.94
  25.1 0.2 fusion.95
  25.3 0.2 fusion.97
  25.6 0.6 gather_fusion
  26.2 0.3 fusion.82
  26.5 0.3 fusion.81
  26.9 0.6 %copy.269 = f32[1,4,2,2,8]{4,2,3,0,1:T(2,128)} copy(f32[1,4,2,2,8]{4,1,3,2,0:T(4,128)S(1)} %bitcast_maximum_fusion) | data formatting | bytes 1024 | tf_op jit(solution)/shard_map/max | solution.py:73
  27.5 4.6 %all-to-all-start.1 = ((f32[1,4,2,2,8]{4,2,3,0,1:T(2,128)}), f32[1,4,2,2,8]{4,2,3,0,1:T(2,128)S(1)}, u32[]{:S(2)}, u32[]{:S(2)}) async-start(f32[1,4,2,2,8]{4,2,3,0,1:T(2,128)} %copy.269), calls=%async_computation.1 | async-start | bytes 16384 | tf_op jit(solution)/shard_map/all_to_all | solution.py:159
  32.1 0.2 fusion.42
  32.3 0.2 convolution_bitcast_fusion.2
  32.5 0.1 copy.264
  32.6 0.1 copy.261
  32.7 0.1 copy.255
  32.9 0.2 fusion.32
  33.1 0.7 %copy-done.9 = bf16[1,2,2,128]{3,2,1,0:T(2,128)(2,1)S(1)} copy-done((bf16[1,2,2,128]{3,2,1,0:T(2,128)(2,1)S(1)}, bf16[1,2,2,128]{3,2,1,0:T(2,128)(2,1)}, u32[]{:S(2)}) %copy-start.9) | copy-done | bytes 1048
  33.8 0.1 convolution_multiply_fusion.5
  34.0 0.1 convert_bitcast_fusion
  34.1 0.2 fusion.19
  34.4 0.3 fusion.18
  34.7 0.2 fusion.27
  34.9 0.6 %copy.265 = f32[1,4,2,2,8,128]{5,4,3,2,0,1:T(8,128)} copy(f32[1,4,2,2,8,128]{5,1,4,3,2,0:T(4,128)S(1)} %fusion.18) | data formatting | bytes 131072 | tf_op jit(solution)/shard_map/broadcast_in_dim | solution.py:161
  35.5 0.6 %copy.285 = f32[1,4,2,2,8]{4,3,2,0,1:T(2,128)} copy(f32[1,4,2,2,8]{4,1,3,2,0:T(4,128)S(1)} %fusion.27) | data formatting | bytes 1024 | tf_op jit(solution)/shard_map/broadcast_in_dim | solution.py:160
  36.1 1.6 %all-to-all-done.1 = f32[1,4,2,2,8]{4,2,3,0,1:T(2,128)S(1)} async-done(((f32[1,4,2,2,8]{4,2,3,0,1:T(2,128)}), f32[1,4,2,2,8]{4,2,3,0,1:T(2,128)S(1)}, u32[]{:S(2)}, u32[]{:S(2)}) %all-to-all-start.1) | async-done | bytes 544 | tf_op jit(solution)/shard_map/all_to_all | solution.py:159
  37.7 3.5 %all-to-all-start.2 = ((f32[1,4,2,2,8]{4,3,2,0,1:T(2,128)}), f32[1,4,2,2,8]{4,3,2,0,1:T(2,128)S(1)}, u32[]{:S(2)}, u32[]{:S(2)}) async-start(f32[1,4,2,2,8]{4,3,2,0,1:T(2,128)} %copy.285), calls=%async_computation.2 | async-start | bytes 16384 | tf_op jit(solution)/shard_map/all_to_all | solution.py:160
  41.2 5.5 %all-to-all-done.2 = f32[1,4,2,2,8]{4,3,2,0,1:T(2,128)S(1)} async-done(((f32[1,4,2,2,8]{4,3,2,0,1:T(2,128)}), f32[1,4,2,2,8]{4,3,2,0,1:T(2,128)S(1)}, u32[]{:S(2)}, u32[]{:S(2)}) %all-to-all-start.2) | async-done | bytes 544 | tf_op jit(solution)/shard_map/all_to_all | solution.py:160
  46.8 3.3 %all-to-all-start = ((f32[1,4,2,2,8,128]{5,4,3,2,0,1:T(8,128)}), f32[1,4,2,2,8,128]{5,4,3,2,0,1:T(8,128)S(1)}, u32[]{:S(2)}, u32[]{:S(2)}) async-start(f32[1,4,2,2,8,128]{5,4,3,2,0,1:T(8,128)} %copy.265), calls=%async_computation | async-start | bytes 131072 | tf_op jit(solution)/shard_map/all_to_all | solution.py:161
  50.1 5.7 %all-to-all-done = f32[1,4,2,2,8,128]{5,4,3,2,0,1:T(8,128)S(1)} async-done(((f32[1,4,2,2,8,128]{5,4,3,2,0,1:T(8,128)}), f32[1,4,2,2,8,128]{5,4,3,2,0,1:T(8,128)S(1)}, u32[]{:S(2)}, u32[]{:S(2)}) %all-to-all-start) | async-done | bytes 65568 | tf_op jit(solution)/shard_map/all_to_all | solution.py:161
  55.9 0.7 %copy-done.10 = bf16[1,2,2,128]{3,2,1,0:T(2,128)(2,1)S(1)} copy-done((bf16[1,2,2,128]{3,2,1,0:T(2,128)(2,1)S(1)}, bf16[1,2,2,128]{3,2,1,0:T(2,128)(2,1)}, u32[]{:S(2)}) %copy-start.10) | copy-done | bytes 1048
  56.5 0.2 fusion.25
  56.7 0.6 %copy.443 = bf16[1,2,2,8,128]{4,3,2,1,0:T(8,128)(2,1)} copy(bf16[1,2,2,8,128]{4,3,1,2,0:T(8,128)(2,1)S(1)} %fusion.25) | data formatting | bytes 16384 | tf_op jit(solution)/shard_map/convert_element_type | solution.py:170
  (56 shorter events, 1.2 us)
Async XLA Ops:
  0.0 34.1 %copy-start = (bf16[256,2,128]{2,1,0:T(2,128)(2,1)S(1)}, bf16[256,2,128]{2,1,0:T(2,128)(2,1)}, u32[]{:S(2)}) copy-start(bf16[256,2,128]{2,1,0:T(2,128)(2,1)} %param.20) | copy-start | bytes 393220
  0.0 0.7 %copy-start.2 = (s32[4]{0:T(128)S(1)}, s32[4]{0:T(128)}, u32[]{:S(2)}) copy-start(s32[4]{0:T(128)} %param.29) | copy-start | bytes 52
  0.0 0.7 %copy-start.3 = (s32[4]{0:T(128)S(1)}, s32[4]{0:T(128)}, u32[]{:S(2)}) copy-start(s32[4]{0:T(128)} %param.28) | copy-start | bytes 52
  0.0 0.9 %copy-start.1 = (bf16[1,2,16,128]{3,2,1,0:T(8,128)(2,1)S(1)}, bf16[1,2,16,128]{3,2,1,0:T(8,128)(2,1)}, u32[]{:S(2)}) copy-start(bf16[1,2,16,128]{3,2,1,0:T(8,128)(2,1)} %param.16) | copy-start | bytes 24580
  15.8 0.7 %copy-start.4 = (s32[4]{0:T(128)S(1)}, s32[4]{0:T(128)}, u32[]{:S(2)}) copy-start(s32[4]{0:T(128)} %param.26) | copy-start | bytes 52
  15.8 0.7 %copy-start.11 = (s32[4]{0:T(128)S(1)}, s32[4]{0:T(128)}, u32[]{:S(2)}) copy-start(s32[4]{0:T(128)} %param.25) | copy-start | bytes 52
  16.5 0.7 %copy-start.5 = (s32[4]{0:T(128)S(1)}, s32[4]{0:T(128)}, u32[]{:S(2)}) copy-start(s32[4]{0:T(128)} %param.27) | copy-start | bytes 52
  18.5 7.7 %copy-start.6 = (bf16[2,128,2,128]{3,2,1,0:T(2,128)(2,1)S(1)}, bf16[2,128,2,128]{3,2,1,0:T(2,128)(2,1)}, u32[]{:S(2)}) copy-start(bf16[2,128,2,128]{3,2,1,0:T(2,128)(2,1)} %param.23) | copy-start | bytes 393220
  25.5 1.0 %copy-start.7 = (bf16[256,2,128]{2,1,0:T(2,128)(2,1)S(1)}, bf16[256,2,128]{2,1,0:T(2,128)(2,1)}, u32[]{:S(2)}) copy-start(bf16[256,2,128]{2,1,0:T(2,128)(2,1)} %param.19) | copy-start | bytes 393220
  26.8 5.5 %copy-start.8 = (bf16[2,128,2,128]{3,2,1,0:T(2,128)(2,1)S(1)}, bf16[2,128,2,128]{3,2,1,0:T(2,128)(2,1)}, u32[]{:S(2)}) copy-start(bf16[2,128,2,128]{3,2,1,0:T(2,128)(2,1)} %param.24) | copy-start | bytes 393220
  27.5 10.2 %all-to-all-start.1 = ((f32[1,4,2,2,8]{4,2,3,0,1:T(2,128)}), f32[1,4,2,2,8]{4,2,3,0,1:T(2,128)S(1)}, u32[]{:S(2)}, u32[]{:S(2)}) async-start(f32[1,4,2,2,8]{4,2,3,0,1:T(2,128)} %copy.269), calls=%async_computation.1 | async-start | bytes 16384 | tf_op jit(solution)/shard_map/all_to_all | solution.py:159
  33.1 0.7 %copy-start.9 = (bf16[1,2,2,128]{3,2,1,0:T(2,128)(2,1)S(1)}, bf16[1,2,2,128]{3,2,1,0:T(2,128)(2,1)}, u32[]{:S(2)}) copy-start(bf16[1,2,2,128]{3,2,1,0:T(2,128)(2,1)} %param.17) | copy-start | bytes 3076
  37.7 9.1 %all-to-all-start.2 = ((f32[1,4,2,2,8]{4,3,2,0,1:T(2,128)}), f32[1,4,2,2,8]{4,3,2,0,1:T(2,128)S(1)}, u32[]{:S(2)}, u32[]{:S(2)}) async-start(f32[1,4,2,2,8]{4,3,2,0,1:T(2,128)} %copy.285), calls=%async_computation.2 | async-start | bytes 16384 | tf_op jit(solution)/shard_map/all_to_all | solution.py:160
  46.8 9.0 %all-to-all-start = ((f32[1,4,2,2,8,128]{5,4,3,2,0,1:T(8,128)}), f32[1,4,2,2,8,128]{5,4,3,2,0,1:T(8,128)S(1)}, u32[]{:S(2)}, u32[]{:S(2)}) async-start(f32[1,4,2,2,8,128]{5,4,3,2,0,1:T(8,128)} %copy.265), calls=%async_computation | async-start | bytes 131072 | tf_op jit(solution)/shard_map/all_to_all | solution.py:161
  55.9 0.7 %copy-start.10 = (bf16[1,2,2,128]{3,2,1,0:T(2,128)(2,1)S(1)}, bf16[1,2,2,128]{3,2,1,0:T(2,128)(2,1)}, u32[]{:S(2)}) copy-start(bf16[1,2,2,128]{3,2,1,0:T(2,128)(2,1)} %param.18) | copy-start | bytes 3076
where the time goes:
time: 57.8 us; the launch traced here: 57.3 us
  blocking collectives  14.9 us (26%)
  waiting for transfers between devices  12.8 us (22%)
  starting transfers between devices  11.4 us (20%)
  local copies, waits for them, and re-layouts  10.6 us (18%)
  other arithmetic  4.6 us (8%)
  matrix products  2.72 us (5%)
    all_gather x1, blocking collectives, per_device(): gathered = lax.all_gather(queries, 'seq', axis=0, tiled=True)  14.9 us
    all_to_all x1, waiting for transfers between devices, per_device(): lax.all_to_all(weighted[None], 'seq', split_axis=1, concat_axis=0, tiled=...  5.66 us
    all_to_all x1, waiting for transfers between devices, per_device(): lax.all_to_all(totals[None], 'seq', split_axis=1, concat_axis=0, tiled=True)  5.54 us
    all_to_all x1, starting transfers between devices, per_device(): lax.all_to_all(highest[None], 'seq', split_axis=1, concat_axis=0, tiled=T...  4.63 us
    dynamic_slice x4, local copies, waits for them, and re-layouts, block_attend(): lax.scan(advance, start_state, (key_blocks, value_blocks, starts))  3.68 us
    all_to_all x1, starting transfers between devices, per_device(): lax.all_to_all(totals[None], 'seq', split_axis=1, concat_axis=0, tiled=True)  3.48 us
    all_to_all x1, starting transfers between devices, per_device(): lax.all_to_all(weighted[None], 'seq', split_axis=1, concat_axis=0, tiled=...  3.28 us
    unnamed x24, local copies, waits for them, and re-layouts  3.18 us
  transfers between devices with their start and end apart: 3, of which 3 were waited for; matrix products, arithmetic and copies ran while one was open for 6% of the time, Pallas kernels for 0%

commit v1 on v0

v1 whole, which is shorter than its diff:
```python
import functools

import jax
import jax.numpy as jnp
from jax import lax
from jax.experimental import pallas as pl
from jax.experimental.pallas import tpu as pltpu
from jax.sharding import PartitionSpec as P

very_low = -1e30


def each(count, step, carry):
    if count <= 8:
        for index in range(count):
            carry = step(index, carry)
        return carry
    return lax.fori_loop(0, count, step, carry)


def attend_kernel(
    sizes,
    q_hbm,
    nk_hbm,
    nv_hbm,
    sk_hbm,
    sv_hbm,
    fk_hbm,
    fv_hbm,
    uk_hbm,
    uv_hbm,
    prefix_hbm,
    owner_hbm,
    plen_hbm,
    slot_hbm,
    slen_hbm,
    out_ref,
    q_own,
    nk_own,
    nv_own,
    k_raw,
    v_raw,
    k_cat,
    v_cat,
    prefix_s,
    owner_s,
    plen_s,
    slot_s,
    slen_s,
    q_got,
    sum_out,
    sum_got,
    stat_out,
    stat_got,
    local_sem,
    q_send,
    q_recv,
    sum_send,
    sum_recv,
    stat_send,
    stat_recv,
):
    n, kv, steps, group, width, shared_len, few_len, slots, suf_len = sizes
    me = lax.axis_index("seq")
    heads = kv * group
    rows = steps * heads
    tiles = rows // 8
    keys = shared_len + few_len + slots * suf_len
    inv_root = width ** (-0.5)

    def peer(distance):
        return lax.rem(me + distance, n)

    barrier = pltpu.get_barrier_semaphore()

    def greet(index, carry):
        pl.semaphore_signal(barrier, inc=1, device_id={"seq": peer(index + 1)})
        return carry

    each(n - 1, greet, 0)

    locals_ = []

    def bring(source, target):
        copy = pltpu.make_async_copy(source, target, local_sem.at[len(locals_)])
        copy.start()
        locals_.append(copy)

    bring(q_hbm, q_own)
    first, second, last = (
        shared_len * kv,
        (shared_len + few_len) * kv,
        keys * kv,
    )
    bring(sk_hbm, k_raw.at[pl.ds(0, first)])
    bring(fk_hbm, k_raw.at[pl.ds(first, second - first)])
    bring(uk_hbm, k_raw.at[pl.ds(second, last - second)])
    bring(sv_hbm, v_raw.at[pl.ds(0, first)])
    bring(fv_hbm, v_raw.at[pl.ds(first, second - first)])
    bring(uv_hbm, v_raw.at[pl.ds(second, last - second)])
    bring(prefix_hbm, prefix_s)
    bring(owner_hbm, owner_s)
    bring(plen_hbm, plen_s)
    bring(slot_hbm, slot_s)
    bring(slen_hbm, slen_s)
    bring(nk_hbm, nk_own)
    bring(nv_hbm, nv_own)

    locals_[0].wait()
    pl.semaphore_wait(barrier, n - 1)

    def query_copy(distance):
        return pltpu.make_async_remote_copy(
            src_ref=q_own,
            dst_ref=q_got.at[distance],
            send_sem=q_send.at[distance],
            recv_sem=q_recv.at[distance],
            device_id={"seq": peer(distance)},
            device_id_type=pl.DeviceIdType.MESH,
        )

    def sum_copy(distance):
        return pltpu.make_async_remote_copy(
            src_ref=sum_out.at[distance],
            dst_ref=sum_got.at[distance],
            send_sem=sum_send.at[distance],
            recv_sem=sum_recv.at[distance],
            device_id={"seq": peer(distance)},
            device_id_type=pl.DeviceIdType.MESH,
        )

    def stat_copy(distance):
        return pltpu.make_async_remote_copy(
            src_ref=stat_out.at[distance],
            dst_ref=stat_got.at[distance],
            send_sem=stat_send.at[distance],
            recv_sem=stat_recv.at[distance],
            device_id={"seq": peer(distance)},
            device_id_type=pl.DeviceIdType.MESH,
        )

    order = (2, 1, 3) if n == 4 else None

    def away(index, near_first):
        if order is None:
            return index + 1
        return (order[1:] + order[:1])[index] if near_first else order[index]

    def send_query(index, carry):
        query_copy(away(index, False)).start()
        return carry

    each(n - 1, send_query, 0)

    block = 256 // kv
    row_id = lax.broadcasted_iota(jnp.int32, (256, 256), 0)
    col_id = lax.broadcasted_iota(jnp.int32, (256, 256), 1)
    source_row = lax.rem(row_id, block) * kv + row_id // block
    sorter = jnp.where(col_id == source_row, 1.0, 0.0).astype(jnp.bfloat16)

    def sort_rows(raw, cat):
        for b in range(keys // block):
            part = jnp.dot(
                sorter, raw[pl.ds(b * 256, 256), :], preferred_element_type=jnp.float32
            ).astype(jnp.bfloat16)
            for h in range(kv):
                cat[pl.ds(b * block, block), pl.ds(h * width, width)] = part[
                    h * block : (h + 1) * block
                ]

    for index in (1, 2, 3):
        locals_[index].wait()
    sort_rows(k_raw, k_cat)
    for index in (4, 5, 6):
        locals_[index].wait()
    sort_rows(v_raw, v_cat)
    for index in range(7, 14):
        locals_[index].wait()

    head_of_row = lax.rem(lax.broadcasted_iota(jnp.int32, (rows, width), 0), heads) // group
    picks = [jnp.where(head_of_row == h, 1.0, 0.0).astype(jnp.bfloat16) for h in range(kv)]
    column = lax.broadcasted_iota(jnp.int32, (1, keys), 1)

    def partial_sums(query, request):
        home = owner_s[prefix_s[request]]
        few = jnp.where(home == me, plen_s[prefix_s[request]], 0)
        limit = jnp.where(column < shared_len, keys, shared_len + few)
        for s in range(slots):
            start = shared_len + few_len + s * suf_len
            length = jnp.where(slot_s[request] == me * slots + s, slen_s[request], 0)
            limit = jnp.where(column >= start, start + length, limit)
        bias = jnp.where(column < limit, 0.0, very_low)
        wide = jnp.concatenate([query * pick for pick in picks], axis=1)
        scores = (
            lax.dot_general(
                wide,
                k_cat[...],
                (((1,), (1,)), ((), ())),
                preferred_element_type=jnp.float32,
            )
            * inv_root
            + bias
        )
        top = jnp.max(scores, axis=1, keepdims=True)
        weights = jnp.exp(scores - top)
        total = jnp.sum(weights, axis=1, keepdims=True)
        both = jnp.dot(
            weights.astype(jnp.bfloat16), v_cat[...], preferred_element_type=jnp.float32
        )
        numer = both[:, :width]
        for h in range(1, kv):
            numer = jnp.where(head_of_row == h, both[:, h * width : (h + 1) * width], numer)
        return top, total, numer

    lane = lax.broadcasted_iota(jnp.int32, (8, 128), 1)

    def pack_stats(top, total):
        packed = jnp.zeros((8, 128), jnp.float32)
        for tile in range(tiles):
            part = slice(tile * 8, tile * 8 + 8)
            packed = jnp.where(lane == tile, top[part], packed)
            packed = jnp.where(lane == tile + tiles, total[part], packed)
        return packed

    own_query = q_own[...]
    own_top, own_total, own_numer = partial_sums(own_query, me)
    fresh = steps * kv
    new_scores = (
        lax.dot_general(
            own_query,
            nk_own[...],
            (((1,), (1,)), ((), ())),
            preferred_element_type=jnp.float32,
        )
        * inv_root
    )
    new_row = lax.broadcasted_iota(jnp.int32, (rows, fresh), 0)
    new_col = lax.broadcasted_iota(jnp.int32, (rows, fresh), 1)
    seen = (lax.rem(new_row, heads) // group == lax.rem(new_col, kv)) & (
        new_col // kv <= new_row // heads
    )
    new_scores = jnp.where(seen, new_scores, very_low)
    joint_top = jnp.maximum(own_top, jnp.max(new_scores, axis=1, keepdims=True))
    old_factor = jnp.exp(own_top - joint_top)
    new_weights = jnp.exp(new_scores - joint_top)
    own_total = own_total * old_factor + jnp.sum(new_weights, axis=1, keepdims=True)
    own_numer = own_numer * old_factor
    rounded = new_weights.astype(jnp.bfloat16).astype(jnp.float32)
    new_values = nv_own[...].astype(jnp.float32)
    for j in range(fresh):
        own_numer = own_numer + rounded[:, j : j + 1] * new_values[j : j + 1, :]
    own_stat = pack_stats(joint_top, own_total)

    def serve(index, carry):
        distance = away(index, True)
        query_copy(distance).wait_recv()
        top, total, numer = partial_sums(q_got[distance], lax.rem(me + n - distance, n))
        back = n - distance
        sum_out[back] = numer.astype(jnp.bfloat16)
        sum_copy(back).start()
        stat_out[back] = pack_stats(top, total)
        stat_copy(back).start()
        return carry

    each(n - 1, serve, 0)

    def find_top(index, highest):
        stat_copy(index + 1).wait_recv()
        return jnp.maximum(highest, stat_got[index + 1])

    highest = each(n - 1, find_top, own_stat)

    def add_total(index, total):
        stat = stat_got[index + 1]
        return total + pltpu.roll(jnp.exp(stat - highest), tiles, 1) * stat

    own_scale = jnp.exp(own_stat - highest)
    total = each(n - 1, add_total, pltpu.roll(own_scale, tiles, 1) * own_stat)
    inverse = 1.0 / jnp.where(lane < tiles, pltpu.roll(total, 128 - tiles, 1), 1.0)

    def spread_rows(scale):
        return jnp.concatenate(
            [jnp.broadcast_to(scale[:, t : t + 1], (8, width)) for t in range(tiles)], axis=0
        )

    def add_sum(index, result):
        sum_copy(index + 1).wait_recv()
        scale = jnp.exp(stat_got[index + 1] - highest) * inverse
        return result + sum_got[index + 1].astype(jnp.float32) * spread_rows(scale)

    result = each(n - 1, add_sum, own_numer * spread_rows(own_scale * inverse))
    out_ref[...] = result.astype(jnp.bfloat16)

    def settle(index, carry):
        query_copy(index + 1).wait_send()
        sum_copy(index + 1).wait_send()
        stat_copy(index + 1).wait_send()
        return carry

    each(n - 1, settle, 0)


def per_device(
    queries,
    new_keys,
    new_values,
    shared_keys,
    shared_values,
    fewshot_keys,
    fewshot_values,
    suffix_keys,
    suffix_values,
    *lists,
):
    n = lax.axis_size("seq")
    steps, heads, width = queries.shape[1:]
    kv = new_keys.shape[2]
    group = heads // kv
    rows = steps * heads
    shared_len, few_len = shared_keys.shape[0], fewshot_keys.shape[0]
    slots, suf_len = suffix_keys.shape[:2]
    keys = shared_len + few_len + slots * suf_len
    sizes = (n, kv, steps, group, width, shared_len, few_len, slots, suf_len)
    flat = [
        item.reshape(-1, width)
        for item in (
            queries,
            new_keys,
            new_values,
            shared_keys,
            shared_values,
            fewshot_keys,
            fewshot_values,
            suffix_keys,
            suffix_values,
        )
    ]
    half, full = jnp.bfloat16, jnp.float32
    dma = pltpu.SemaphoreType.DMA
    result = pl.pallas_call(
        functools.partial(attend_kernel, sizes),
        out_shape=jax.ShapeDtypeStruct((rows, width), half),
        in_specs=[pl.BlockSpec(memory_space=pltpu.HBM)] * 14,
        out_specs=pl.BlockSpec(memory_space=pltpu.VMEM),
        scratch_shapes=[
            pltpu.VMEM((rows, width), half),
            pltpu.VMEM((steps * kv, width), half),
            pltpu.VMEM((steps * kv, width), half),
            pltpu.VMEM((keys * kv, width), half),
            pltpu.VMEM((keys * kv, width), half),
            pltpu.VMEM((keys, kv * width), half),
            pltpu.VMEM((keys, kv * width), half),
        ]
        + [pltpu.SMEM(item.shape, jnp.int32) for item in lists]
        + [
            pltpu.VMEM((n, rows, width), half),
            pltpu.VMEM((n, rows, width), half),
            pltpu.VMEM((n, rows, width), half),
            pltpu.VMEM((n, 8, 128), full),
            pltpu.VMEM((n, 8, 128), full),
            dma((14,)),
        ]
        + [dma((n,))] * 6,
        compiler_params=pltpu.CompilerParams(collective_id=0, has_side_effects=True),
        name="prefix_attend",
    )(*flat, *lists)
    return result.reshape(queries.shape)


def solution(mesh):
    seq_rows = P(("groups", "seq"), None, "head", None)
    seq_keys = P(("groups", "seq"), "head", None)
    return jax.shard_map(
        per_device,
        mesh=mesh,
        in_specs=(seq_rows,) * 3 + (seq_keys,) * 4 + (seq_rows,) * 2 + (P("groups"),) * 5,
        out_specs=seq_rows,
        check_vma=False,
    )
```

time: 57.8 us -> 16 us (0.28)
  blocking collectives: 14.9 us -> 0 us
  Pallas kernels: 0 us -> 14.4 us
  waiting for transfers between devices: 12.8 us -> 0 us
  starting transfers between devices: 11.4 us -> 0 us
  local copies, waits for them, and re-layouts: 10.6 us -> 1.3 us
  other arithmetic: 4.6 us -> 0 us
  matrix products: 2.72 us -> 0 us
    all_gather x1 -> x0, blocking collectives: 14.9 us -> none  [per_device(): gathered = lax.all_gather(queries, 'seq', axis=0, tiled=True)]
    pallas_call x0 -> x1, Pallas kernels: none -> 14.4 us  [per_device(): pl.pallas_call(functools.partial(attend_kernel, sizes), out_shape=jax.Sha...]
    all_to_all x3 -> x0, waiting for transfers between devices: 12.8 us -> none  [the longest x1 5.66 us: per_device(): lax.all_to_all(weighted[None], 'seq', split_axis=1, concat_axis=0, tiled=...]
    all_to_all x3 -> x0, starting transfers between devices: 11.4 us -> none  [the longest x1 4.63 us: per_device(): lax.all_to_all(highest[None], 'seq', split_axis=1, concat_axis=0, tiled=T...]
    dynamic_slice x4 -> x0, local copies, waits for them, and re-layouts: 3.68 us -> none  [block_attend(): lax.scan(advance, start_state, (key_blocks, value_blocks, starts))]
    dot_general x12 -> x0, matrix products: 2.72 us -> none  [the longest x3 0.76 us: advance(): jnp.einsum('bgqd,lgd->bgql', rows_in, key_part, preferred_element_type=jn...]
    unnamed x24 -> x1, local copies, waits for them, and re-layouts: 3.18 us -> 1.3 us
    reduce_sum x9 -> x0, other arithmetic: 1.87 us -> none  [the longest x1 0.71 us: per_device(): own_length = jnp.sum(jnp.where(prefix_owner == my_index, prefix_length, 0))]
  transfers between devices with their start and end apart: 3 -> 0, of which waited for: 3 -> 0; matrix products, arithmetic and copies ran while one was open for 6% -> 0% of each run, Pallas kernels for 0% -> 0%
where the time goes in v1:
time: 16 us; the launch traced here: 15.8 us
  Pallas kernels  14.4 us (90%)
  local copies, waits for them, and re-layouts  1.3 us (8%)
    pallas_call x1, Pallas kernels, per_device(): pl.pallas_call(functools.partial(attend_kernel, sizes), out_shape=jax.Sha...  14.4 us
    unnamed x1, local copies, waits for them, and re-layouts  1.3 us

profile of v1, /device:TPU:0, one launch (start us, length us, event | category | flops | bytes accessed | tf_op | source)
XLA Modules:
  0.0 15.8 jit_solution(3171118571074682778)
XLA Ops:
  0.0 14.4 %prefix_attend.1 = bf16[32,128]{1,0:T(8,128)(2,1)} custom-call(bf16[32,128]{1,0:T(8,128)(2,1)} %bitcast.17, bf16[4,128]{1,0:T(4,128)(2,1)} %bitcast.18, bf16[4,128]{1,0:T(4,128)(2,1)} %bitcast.19, bf16[512,128]{1,0:T(8,128)(2,1)} %bitcast.12, bf16[512,128]{1,0:T(8,128)(2,1)} %bitcast.13, bf16[1024,128]{1,0:T(8,128)(2,1)} %bitcast.10, ...), custom_call_target="tpu_custom_call" | custom-call | tf_op jit(solution)/shard_map/prefix_attend/pallas_call | solution.py:340
  14.5 1.3 %copy.16 = bf16[1,2,16,128]{3,2,1,0:T(8,128)(2,1)} copy(bf16[1,2,16,128]{3,2,1,0:T(8,128)(2,1)} %bitcast.16) | data formatting | bytes 16384

commit v2 on v1

--- a/solution.py
+++ b/solution.py
@@ -35,7 +35,6 @@
     slot_hbm,
     slen_hbm,
     out_ref,
-    q_own,
     nk_own,
     nv_own,
     k_raw,
@@ -52,6 +51,7 @@
     sum_got,
     stat_out,
     stat_got,
+    bias_rows,
     local_sem,
     q_send,
     q_recv,
@@ -86,7 +86,7 @@
         copy.start()
         locals_.append(copy)
 
-    bring(q_hbm, q_own)
+    bring(q_hbm, q_got.at[0])
     first, second, last = (
         shared_len * kv,
         (shared_len + few_len) * kv,
@@ -111,7 +111,7 @@
 
     def query_copy(distance):
         return pltpu.make_async_remote_copy(
-            src_ref=q_own,
+            src_ref=q_got.at[0],
             dst_ref=q_got.at[distance],
             send_sem=q_send.at[distance],
             recv_sem=q_recv.at[distance],
@@ -139,15 +139,8 @@
             device_id_type=pl.DeviceIdType.MESH,
         )
 
-    order = (2, 1, 3) if n == 4 else None
-
-    def away(index, near_first):
-        if order is None:
-            return index + 1
-        return (order[1:] + order[:1])[index] if near_first else order[index]
-
     def send_query(index, carry):
-        query_copy(away(index, False)).start()
+        query_copy(index + 1).start()
         return carry
 
     each(n - 1, send_query, 0)
@@ -168,20 +161,11 @@
                     h * block : (h + 1) * block
                 ]
 
-    for index in (1, 2, 3):
-        locals_[index].wait()
-    sort_rows(k_raw, k_cat)
-    for index in (4, 5, 6):
-        locals_[index].wait()
-    sort_rows(v_raw, v_cat)
     for index in range(7, 14):
         locals_[index].wait()
-
-    head_of_row = lax.rem(lax.broadcasted_iota(jnp.int32, (rows, width), 0), heads) // group
-    picks = [jnp.where(head_of_row == h, 1.0, 0.0).astype(jnp.bfloat16) for h in range(kv)]
     column = lax.broadcasted_iota(jnp.int32, (1, keys), 1)
 
-    def partial_sums(query, request):
+    def mask_row(request, carry):
         home = owner_s[prefix_s[request]]
         few = jnp.where(home == me, plen_s[prefix_s[request]], 0)
         limit = jnp.where(column < shared_len, keys, shared_len + few)
@@ -189,8 +173,69 @@
             start = shared_len + few_len + s * suf_len
             length = jnp.where(slot_s[request] == me * slots + s, slen_s[request], 0)
             limit = jnp.where(column >= start, start + length, limit)
-        bias = jnp.where(column < limit, 0.0, very_low)
-        wide = jnp.concatenate([query * pick for pick in picks], axis=1)
+        bias_rows[pl.ds(request, 1), :] = jnp.where(column < limit, 0.0, very_low)
+        return carry
+
+    each(n, mask_row, 0)
+
+    for index in (1, 2, 3):
+        locals_[index].wait()
+    sort_rows(k_raw, k_cat)
+    for index in (4, 5, 6):
+        locals_[index].wait()
+    sort_rows(v_raw, v_cat)
+
+    head_of_row = lax.rem(lax.broadcasted_iota(jnp.int32, (rows, width), 0), heads) // group
+    picks = [jnp.where(head_of_row == h, 1.0, 0.0).astype(jnp.bfloat16) for h in range(kv)]
+    lane = lax.broadcasted_iota(jnp.int32, (8, 128), 1)
+
+    def pack_stats(top, total):
+        packed = jnp.zeros((8, 128), jnp.float32)
+        for tile in range(tiles):
+            part = slice(tile * 8, tile * 8 + 8)
+            packed = jnp.where(lane == tile, top[part], packed)
+            packed = jnp.where(lane == tile + tiles, total[part], packed)
+        return packed
+
+    own_query = q_got[0]
+    fresh = steps * kv
+    new_scores = (
+        lax.dot_general(
+            own_query,
+            nk_own[...],
+            (((1,), (1,)), ((), ())),
+            preferred_element_type=jnp.float32,
+        )
+        * inv_root
+    )
+    new_row = lax.broadcasted_iota(jnp.int32, (rows, fresh), 0)
+    new_col = lax.broadcasted_iota(jnp.int32, (rows, fresh), 1)
+    seen = (lax.rem(new_row, heads) // group == lax.rem(new_col, kv)) & (
+        new_col // kv <= new_row // heads
+    )
+    new_scores = jnp.where(seen, new_scores, very_low)
+    new_top = jnp.max(new_scores, axis=1, keepdims=True)
+    new_weights = jnp.exp(new_scores - new_top)
+    rounded = new_weights.astype(jnp.bfloat16).astype(jnp.float32)
+    new_values = nv_own[...].astype(jnp.float32)
+    new_numer = jnp.zeros((rows, width), jnp.float32)
+    for j in range(fresh):
+        new_numer = new_numer + rounded[:, j : j + 1] * new_values[j : j + 1, :]
+    new_stat = pack_stats(new_top, jnp.sum(new_weights, axis=1, keepdims=True))
+
+    def distance_from(request):
+        return lax.rem(me + n - request, n)
+
+    def serve(request, carry):
+        distance = distance_from(request)
+        back = lax.rem(request + n - me, n)
+        remote = distance != 0
+
+        @pl.when(remote)
+        def _():
+            query_copy(distance).wait_recv()
+
+        wide = jnp.concatenate([q_got[distance] * pick for pick in picks], axis=1)
         scores = (
             lax.dot_general(
                 wide,
@@ -199,97 +244,70 @@
                 preferred_element_type=jnp.float32,
             )
             * inv_root
-            + bias
+            + bias_rows[pl.ds(request, 1), :]
         )
         top = jnp.max(scores, axis=1, keepdims=True)
         weights = jnp.exp(scores - top)
         total = jnp.sum(weights, axis=1, keepdims=True)
+        stat_out[back] = pack_stats(top, total)
+
+        @pl.when(remote)
+        def _():
+            stat_copy(back).start()
+
         both = jnp.dot(
             weights.astype(jnp.bfloat16), v_cat[...], preferred_element_type=jnp.float32
         )
         numer = both[:, :width]
         for h in range(1, kv):
             numer = jnp.where(head_of_row == h, both[:, h * width : (h + 1) * width], numer)
-        return top, total, numer
-
-    lane = lax.broadcasted_iota(jnp.int32, (8, 128), 1)
-
-    def pack_stats(top, total):
-        packed = jnp.zeros((8, 128), jnp.float32)
-        for tile in range(tiles):
-            part = slice(tile * 8, tile * 8 + 8)
-            packed = jnp.where(lane == tile, top[part], packed)
-            packed = jnp.where(lane == tile + tiles, total[part], packed)
-        return packed
-
-    own_query = q_own[...]
-    own_top, own_total, own_numer = partial_sums(own_query, me)
-    fresh = steps * kv
-    new_scores = (
-        lax.dot_general(
-            own_query,
-            nk_own[...],
-            (((1,), (1,)), ((), ())),
-            preferred_element_type=jnp.float32,
-        )
-        * inv_root
-    )
-    new_row = lax.broadcasted_iota(jnp.int32, (rows, fresh), 0)
-    new_col = lax.broadcasted_iota(jnp.int32, (rows, fresh), 1)
-    seen = (lax.rem(new_row, heads) // group == lax.rem(new_col, kv)) & (
-        new_col // kv <= new_row // heads
-    )
-    new_scores = jnp.where(seen, new_scores, very_low)
-    joint_top = jnp.maximum(own_top, jnp.max(new_scores, axis=1, keepdims=True))
-    old_factor = jnp.exp(own_top - joint_top)
-    new_weights = jnp.exp(new_scores - joint_top)
-    own_total = own_total * old_factor + jnp.sum(new_weights, axis=1, keepdims=True)
-    own_numer = own_numer * old_factor
-    rounded = new_weights.astype(jnp.bfloat16).astype(jnp.float32)
-    new_values = nv_own[...].astype(jnp.float32)
-    for j in range(fresh):
-        own_numer = own_numer + rounded[:, j : j + 1] * new_values[j : j + 1, :]
-    own_stat = pack_stats(joint_top, own_total)
-
-    def serve(index, carry):
-        distance = away(index, True)
-        query_copy(distance).wait_recv()
-        top, total, numer = partial_sums(q_got[distance], lax.rem(me + n - distance, n))
-        back = n - distance
         sum_out[back] = numer.astype(jnp.bfloat16)
-        sum_copy(back).start()
-        stat_out[back] = pack_stats(top, total)
-        stat_copy(back).start()
-        return carry
-
-    each(n - 1, serve, 0)
+
+        @pl.when(remote)
+        def _():
+            sum_copy(back).start()
+
+        return carry
+
+    each(n, serve, 0)
+
+    def source_of(index):
+        return distance_from(index + jnp.where(index >= me, 1, 0))
+
+    own_stat = stat_out[0]
 
     def find_top(index, highest):
-        stat_copy(index + 1).wait_recv()
-        return jnp.maximum(highest, stat_got[index + 1])
-
-    highest = each(n - 1, find_top, own_stat)
+        slot = source_of(index)
+        stat_copy(slot).wait_recv()
+        return jnp.maximum(highest, stat_got[slot])
+
+    highest = each(n - 1, find_top, jnp.maximum(own_stat, new_stat))
+
+    def share(stat):
+        return pltpu.roll(jnp.exp(stat - highest), tiles, 1) * stat
 
     def add_total(index, total):
-        stat = stat_got[index + 1]
-        return total + pltpu.roll(jnp.exp(stat - highest), tiles, 1) * stat
-
-    own_scale = jnp.exp(own_stat - highest)
-    total = each(n - 1, add_total, pltpu.roll(own_scale, tiles, 1) * own_stat)
+        return total + share(stat_got[source_of(index)])
+
+    total = each(n - 1, add_total, share(own_stat) + share(new_stat))
     inverse = 1.0 / jnp.where(lane < tiles, pltpu.roll(total, 128 - tiles, 1), 1.0)
 
-    def spread_rows(scale):
+    def spread_rows(stat):
+        scale = jnp.exp(stat - highest) * inverse
         return jnp.concatenate(
             [jnp.broadcast_to(scale[:, t : t + 1], (8, width)) for t in range(tiles)], axis=0
         )
 
     def add_sum(index, result):
-        sum_copy(index + 1).wait_recv()
-        scale = jnp.exp(stat_got[index + 1] - highest) * inverse
-        return result + sum_got[index + 1].astype(jnp.float32) * spread_rows(scale)
-
-    result = each(n - 1, add_sum, own_numer * spread_rows(own_scale * inverse))
-    out_ref[...] = result.astype(jnp.bfloat16)
+        slot = source_of(index)
+        scale = spread_rows(stat_got[slot])
+        sum_copy(slot).wait_recv()
+        return result + sum_got[slot].astype(jnp.float32) * scale
+
+    start = new_numer * spread_rows(new_stat) + sum_out[0].astype(jnp.float32) * spread_rows(
+        own_stat
+    )
+    out_ref[...] = each(n - 1, add_sum, start).astype(jnp.bfloat16)
 
     def settle(index, carry):
         query_copy(index + 1).wait_send()
@@ -339,11 +357,10 @@
     dma = pltpu.SemaphoreType.DMA
     result = pl.pallas_call(
         functools.partial(attend_kernel, sizes),
-        out_shape=jax.ShapeDtypeStruct((rows, width), half),
+        out_shape=pltpu.VMEM((rows, width), half),
         in_specs=[pl.BlockSpec(memory_space=pltpu.HBM)] * 14,
         out_specs=pl.BlockSpec(memory_space=pltpu.VMEM),
         scratch_shapes=[
-            pltpu.VMEM((rows, width), half),
             pltpu.VMEM((steps * kv, width), half),
             pltpu.VMEM((steps * kv, width), half),
             pltpu.VMEM((keys * kv, width), half),
@@ -358,6 +375,7 @@
             pltpu.VMEM((n, rows, width), half),
             pltpu.VMEM((n, 8, 128), full),
             pltpu.VMEM((n, 8, 128), full),
+            pltpu.VMEM((n, keys), full),
             dma((14,)),
         ]
         + [dma((n,))] * 6,

time: 16 us -> 14.3 us (0.89)
  Pallas kernels: 14.4 us -> 13.5 us
  local copies, waits for them, and re-layouts: 1.3 us -> 0.6 us
    pallas_call x1, Pallas kernels: 14.4 us -> 13.5 us  [per_device(): pl.pallas_call(functools.partial(attend_kernel, sizes), out_shape=pltpu.V...]
    unnamed x1, local copies, waits for them, and re-layouts: 1.3 us -> 0.6 us
where the time goes in v2:
time: 14.3 us; the launch traced here: 14.1 us
  Pallas kernels  13.5 us (94%)
  local copies, waits for them, and re-layouts  0.6 us (4%)
    pallas_call x1, Pallas kernels, per_device(): pl.pallas_call(functools.partial(attend_kernel, sizes), out_shape=pltpu.V...  13.5 us
    unnamed x1, local copies, waits for them, and re-layouts  0.6 us

profile of v2, /device:TPU:0, one launch (start us, length us, event | category | flops | bytes accessed | tf_op | source)
XLA Modules:
  0.0 14.1 jit_solution(14792656113240832115)
XLA Ops:
  0.0 13.5 %prefix_attend.1 = bf16[32,128]{1,0:T(8,128)(2,1)S(1)} custom-call(bf16[32,128]{1,0:T(8,128)(2,1)} %bitcast.17, bf16[4,128]{1,0:T(4,128)(2,1)} %bitcast.18, bf16[4,128]{1,0:T(4,128)(2,1)} %bitcast.19, bf16[512,128]{1,0:T(8,128)(2,1)} %bitcast.13, bf16[512,128]{1,0:T(8,128)(2,1)} %bitcast.14, bf16[1024,128]{1,0:T(8,128)(2,1)} %bitcast.11, ...), custom_call_target="tpu_custom_call" | custom-call | tf_op jit(solution)/shard_map/prefix_attend/pallas_call | solution.py:358
  13.5 0.6 %copy.16 = bf16[1,2,16,128]{3,2,1,0:T(8,128)(2,1)} copy(bf16[1,2,16,128]{3,2,1,0:T(8,128)(2,1)S(1)} %bitcast.10) | data formatting | bytes 16384

commit v3 on v2

--- a/solution.py
+++ b/solution.py
@@ -113,7 +113,7 @@
         return pltpu.make_async_remote_copy(
             src_ref=q_got.at[0],
             dst_ref=q_got.at[distance],
-            send_sem=q_send.at[distance],
+            send_sem=q_send.at[0],
             recv_sem=q_recv.at[distance],
             device_id={"seq": peer(distance)},
             device_id_type=pl.DeviceIdType.MESH,
@@ -123,7 +123,7 @@
         return pltpu.make_async_remote_copy(
             src_ref=sum_out.at[distance],
             dst_ref=sum_got.at[distance],
-            send_sem=sum_send.at[distance],
+            send_sem=sum_send.at[0],
             recv_sem=sum_recv.at[distance],
             device_id={"seq": peer(distance)},
             device_id_type=pl.DeviceIdType.MESH,
@@ -133,7 +133,7 @@
         return pltpu.make_async_remote_copy(
             src_ref=stat_out.at[distance],
             dst_ref=stat_got.at[distance],
-            send_sem=stat_send.at[distance],
+            send_sem=stat_send.at[0],
             recv_sem=stat_recv.at[distance],
             device_id={"seq": peer(distance)},
             device_id_type=pl.DeviceIdType.MESH,
@@ -309,13 +309,9 @@
     )
     out_ref[...] = each(n - 1, add_sum, start).astype(jnp.bfloat16)
 
-    def settle(index, carry):
-        query_copy(index + 1).wait_send()
-        sum_copy(index + 1).wait_send()
-        stat_copy(index + 1).wait_send()
-        return carry
-
-    each(n - 1, settle, 0)
+    for sent, sem in ((sum_got, q_send), (sum_out, sum_send), (stat_out, stat_send)):
+        part = sent.at[pl.ds(1, n - 1)]
+        pltpu.make_async_copy(part, part, sem.at[0]).wait()
 
 
 def per_device(
@@ -378,7 +374,7 @@
             pltpu.VMEM((n, keys), full),
             dma((14,)),
         ]
-        + [dma((n,))] * 6,
+        + [dma((1,)), dma((n,))] * 3,
         compiler_params=pltpu.CompilerParams(collective_id=0, has_side_effects=True),
         name="prefix_attend",
     )(*flat, *lists)

time: 14.3 us -> 14.2 us (level)
  no operation moved by 1% of the time
where the time goes in v3:
time: 14.2 us; the launch traced here: 14 us
  Pallas kernels  13.4 us (94%)
  local copies, waits for them, and re-layouts  0.6 us (4%)
    pallas_call x1, Pallas kernels, per_device(): pl.pallas_call(functools.partial(attend_kernel, sizes), out_shape=pltpu.V...  13.4 us
    unnamed x1, local copies, waits for them, and re-layouts  0.6 us

profile of v3, /device:TPU:0, one launch (start us, length us, event | category | flops | bytes accessed | tf_op | source)
XLA Modules:
  0.0 14.0 jit_solution(723950263643454910)
XLA Ops:
  0.0 13.4 %prefix_attend.1 = bf16[32,128]{1,0:T(8,128)(2,1)S(1)} custom-call(bf16[32,128]{1,0:T(8,128)(2,1)} %bitcast.17, bf16[4,128]{1,0:T(4,128)(2,1)} %bitcast.18, bf16[4,128]{1,0:T(4,128)(2,1)} %bitcast.19, bf16[512,128]{1,0:T(8,128)(2,1)} %bitcast.13, bf16[512,128]{1,0:T(8,128)(2,1)} %bitcast.14, bf16[1024,128]{1,0:T(8,128)(2,1)} %bitcast.11, ...), custom_call_target="tpu_custom_call" | custom-call | tf_op jit(solution)/shard_map/prefix_attend/pallas_call | solution.py:354
  13.4 0.6 %copy.16 = bf16[1,2,16,128]{3,2,1,0:T(8,128)(2,1)} copy(bf16[1,2,16,128]{3,2,1,0:T(8,128)(2,1)S(1)} %bitcast.10) | data formatting | bytes 16384
